TPU v7x, 512 devices: a whole 4x4x16 slice. The times are simulated.
512 devices in a mesh: row: 16 (over y, x), col: 32 (over z, core).
Axes of the slice: x: 4, y: 4, z: 16, core: 2. Of those that a mesh axis runs over, the one named last changes fastest.
Arguments:
- inverse_sep: float32 [12288, 12288], P('row', 'col'), may hold values from -105 to 105, as said below
- sep_panels: float32 [3, 12288, 256], P(None, 'row', 'col'), may hold values from -0.0546875 to 0.0546875
- chain_panels: float32 [3, 256, 256], P(None, 'row', 'col'), may hold values from -0.375 to 0.375
- diag_inverse: float32 [3, 256, 256], P(None, 'row'), may hold values from -5 to 5, as said below
- tile_list: int32 [3, 96], replicated, may hold values from 0 to 1, as said below
Outputs:
- sep_rows: float32 [3, 256, 12288], P(None, 'row', 'col')
- chain_inverse: float32 [3, 256, 768], P(None, 'row')
Inputs may be any that keep to these rules, and one draw needn't show every extreme that they name: `inverse_sep`: symmetric. `diag_inverse`: each block symmetric. `tile_list`: a tile listed for supernode k is listed for every earlier supernode.
All inputs are finite; a program needn't handle non-finite values.
Results may differ from a plain program's by a relative error of at most 0.00013.
Values sent between devices are 32-bit elements; how exact they have to be, the bound alone decides.
No kernel may reach another device: no remote copies, remote signals or barrier semaphores. Data moves between devices by JAX's collectives and lax.ppermute only.
A program may use at most 64 MiB of HBM per device.

v0:
```python
import jax
import jax.numpy as jnp
from jax import lax
from jax.sharding import PartitionSpec as P

NB = 256
TILE = 128
NSUPER = 3


def broadcast(block, axis, source):
    block = jnp.where(lax.axis_index(axis) == source, block, jnp.zeros_like(block))
    return lax.psum(block, axis)


def pair_index(current, earlier):
    return current * (current - 1) // 2 + earlier


def product(left, right):
    return jnp.dot(left, right, precision=lax.Precision.HIGHEST, preferred_element_type=jnp.float32)


def inner_product(left, right):
    return lax.dot_general(
        left,
        right,
        (((0,), (0,)), ((), ())),
        precision=lax.Precision.HIGHEST,
        preferred_element_type=jnp.float32,
    )


def per_device(inverse_sep, sep_panels, chain_panels, diag_inverse, tile_list):
    row_count = lax.axis_size("row")
    col_count = lax.axis_size("col")
    row_place = lax.axis_index("row")
    col_place = lax.axis_index("col")
    row_cells, col_cells = inverse_sep.shape
    nb_rows = NB // row_count
    nb_cols = NB // col_count
    ratio_cols = col_count // row_count
    root_row = col_place // ratio_cols
    inner_part = col_place % ratio_cols
    tile_rows = row_cells // TILE
    listed = lax.dynamic_slice_in_dim(tile_list, row_place * tile_rows, tile_rows, 1).astype(
        jnp.float32
    )
    panels = [None] * NSUPER
    column_panels = [None] * NSUPER
    chain_rowlay = [None] * NSUPER
    chain_colrows = [None] * NSUPER
    state = jnp.zeros((NSUPER, nb_rows, NSUPER * NB), jnp.float32)
    new_rows = []
    for current in range(NSUPER):
        gathered, chains = (
            lax.all_gather(sep_panels[current : current + 1], "col", axis=2, tiled=True),
            lax.all_gather(chain_panels[current : current + 1], "col", axis=2, tiled=True),
        )
        panels[current] = (
            gathered[0].reshape(tile_rows, TILE, NB) * listed[current][:, None, None]
        ).reshape(row_cells, NB)
        chain_rowlay[current] = chains[0]
        local_col = lax.dynamic_slice_in_dim(panels[current], inner_part * col_cells, col_cells, 0)
        payload = jnp.concatenate(
            [local_col, lax.dynamic_slice_in_dim(chains[0], inner_part * nb_cols, nb_cols, 0)],
            axis=0,
        )
        shared = broadcast(payload, "row", root_row)
        column_panels[current] = shared[:col_cells]
        chain_colrows[current] = shared[col_cells:]
        panel = panels[current]
        earlier_pairs = [
            (chain_rowlay[pair_index(current, earlier)], new_rows[earlier])
            for earlier in range(current)
        ]
        summed = inner_product(panel, inverse_sep)
        for chain_block, old_rows in earlier_pairs:
            summed = summed + inner_product(chain_block, old_rows)
        rows_now = -lax.psum_scatter(summed, "row", scatter_dimension=0, tiled=True)
        col_panel = column_panels[current]
        parts = [product(rows_now, col_panel)]
        for earlier in range(current):
            crossed = product(new_rows[earlier], col_panel)
            for middle in range(current):
                state_cols = lax.dynamic_slice_in_dim(
                    state[earlier], middle * NB + col_place * nb_cols, nb_cols, 1
                )
                crossed = crossed + product(state_cols, chain_colrows[pair_index(current, middle)])
            parts.append(crossed)
        totals = lax.psum(jnp.stack(parts), "col")
        first_term = totals[0]
        crossing = [-totals[1 + earlier] for earlier in range(current)]
        second_term = jnp.zeros((nb_rows, NB), jnp.float32)
        if current > 0:
            mirrored = jnp.swapaxes(
                lax.all_to_all(jnp.stack(crossing), "row", split_axis=2, concat_axis=1, tiled=True),
                1,
                2,
            )
            partial_sum = jnp.zeros((nb_rows, NB), jnp.float32)
            for earlier in range(current):
                mirror_cols = lax.dynamic_slice_in_dim(
                    mirrored[earlier], col_place * nb_cols, nb_cols, 1
                )
                partial_sum = partial_sum + product(
                    mirror_cols, chain_colrows[pair_index(current, earlier)]
                )
            second_term = lax.psum(partial_sum, "col")
            for earlier in range(current):
                state = state.at[earlier, :, current * NB : (current + 1) * NB].set(
                    crossing[earlier]
                )
                state = state.at[current, :, earlier * NB : (earlier + 1) * NB].set(
                    mirrored[earlier]
                )
        state = state.at[current, :, current * NB : (current + 1) * NB].set(
            diag_inverse[current] - first_term - second_term
        )
        new_rows.append(rows_now)
    return (jnp.stack(new_rows), state)


def solution(mesh):
    in_specs = (
        P("row", "col"),
        P(None, "row", "col"),
        P(None, "row", "col"),
        P(None, "row", None),
        P(),
    )
    out_specs = (P(None, "row", "col"), P(None, "row", None))
    return jax.shard_map(
        per_device, mesh=mesh, in_specs=in_specs, out_specs=out_specs, check_vma=False
    )
```

profile of v0, /device:TPU:2, one launch (start us, length us, event | category | flops | bytes accessed | tf_op | source)
XLA Modules:
  0.0 955.0 jit_solution(4085583582345847917)
XLA Ops:
  9.5 38.4 %all_gather.18 = f32[1,768,256]{1,2,0:T(8,128)S(1)} all-gather(f32[1,768,8]{1,2,0:T(8,128)S(1)} %get-tuple-element.119), channel_id=1, replica_groups=mesh['row'=16,'col'=32] {'col'}, dimensions={2}, use_global_device_ids=true | all-gather | bytes 811008 | tf_op jit(solution)/shard_map/all_gather | solution.py:57
  48.0 2.2 fusion.82
  50.3 29.2 %all_gather.21 = f32[1,768,256]{1,2,0:T(8,128)S(1)} all-gather(f32[1,768,8]{1,2,0:T(8,128)S(1)} %get-tuple-element.120), channel_id=1, replica_groups=mesh['row'=16,'col'=32] {'col'}, dimensions={2}, use_global_device_ids=true | all-gather | bytes 811008 | tf_op jit(solution)/shard_map/all_gather | solution.py:57
  79.6 2.2 fusion.84
  81.9 31.4 %all_gather.22 = f32[1,16,256]{1,2,0:T(8,128)} all-gather(f32[1,16,8]{1,2,0:T(8,128)S(1)} %get-tuple-element.131), channel_id=1, replica_groups=mesh['row'=16,'col'=32] {'col'}, dimensions={2}, use_global_device_ids=true | all-gather | bytes 16896 | tf_op jit(solution)/shard_map/all_gather | solution.py:58
  113.3 30.1 %all_gather.23 = f32[1,16,256]{1,2,0:T(8,128)} all-gather(f32[1,16,8]{1,2,0:T(8,128)S(1)} %get-tuple-element.130), channel_id=1, replica_groups=mesh['row'=16,'col'=32] {'col'}, dimensions={2}, use_global_device_ids=true | all-gather | bytes 16896 | tf_op jit(solution)/shard_map/all_gather | solution.py:58
  143.4 30.5 %all_gather.19 = f32[1,768,256]{1,2,0:T(8,128)S(1)} all-gather(f32[1,768,8]{1,2,0:T(8,128)S(1)} %copy-done.9), channel_id=1, replica_groups=mesh['row'=16,'col'=32] {'col'}, dimensions={2}, use_global_device_ids=true | all-gather | bytes 811008 | tf_op jit(solution)/shard_map/all_gather | solution.py:57
  174.0 30.1 %all_gather.20 = f32[1,16,256]{1,2,0:T(8,128)} all-gather(f32[1,16,8]{1,2,0:T(8,128)S(1)} %get-tuple-element.129), channel_id=1, replica_groups=mesh['row'=16,'col'=32] {'col'}, dimensions={2}, use_global_device_ids=true | all-gather | bytes 16896 | tf_op jit(solution)/shard_map/all_gather | solution.py:58
  210.2 1.9 maximum_select_fusion
  214.6 2.0 fusion.2
  218.8 109.7 %all-reduce.11.cloned.1.call-done = f32[256,384]{1,0:T(8,128)} async-done(((f32[256,384]{1,0:T(8,128)}), f32[256,384]{1,0:T(8,128)}) %all-reduce.11.cloned.1.call-update) | async-done | bytes 393232
  328.6 1.9 fusion
  331.2 3.2 and_reduce_fusion
  335.9 117.2 %all-reduce.13.cloned.1.call-done = (f32[256,384]{1,0:T(8,128)}, f32[392,256]{0,1:T(8,128)}, f32[392,256]{0,1:T(8,128)}, f32[392,256]{0,1:T(8,128)}) async-done(((f32[256,384]{1,0:T(8,128)}, f32[392,256]{0,1:T(8,128)}, f32[392,256]{0,1:T(8,128)}, f32[392,256]{0,1:T(8,128)}), (f32[256,384]{1,0:T(8,128)}, f32[392,256]{0,1:T(8,128)}, f32[392,256]{0,1:T(8,128)}, ...) | async-done | bytes 1597456
  454.6 91.6 %psum.57 = f32[1,16,256]{2,1,0:T(8,128)S(1)} all-reduce(f32[1,16,256]{2,1,0:T(8,128)S(1)} %convolution_bitcast_fusion.5), channel_id=1, replica_groups=mesh['row'=16,'col'=32] {'col'}, use_global_device_ids=true, to_apply=%region_4.5 | all-reduce | flops 4096 | bytes 32768 | tf_op jit(solution)/shard_map/psum | solution.py:91
  549.9 90.0 %psum.59 = f32[2,16,256]{2,1,0:T(8,128)S(1)} all-reduce(f32[2,16,256]{2,1,0:T(8,128)S(1)} %pad_maximum_fusion.2), channel_id=1, replica_groups=mesh['row'=16,'col'=32] {'col'}, use_global_device_ids=true, to_apply=%region_7.8 | all-reduce | flops 8192 | bytes 65536 | tf_op jit(solution)/shard_map/psum | solution.py:91
  640.0 2.0 slice_negate_fusion.2
  644.3 5.8 all-to-all-start
  658.6 90.0 %psum.60 = f32[16,256]{1,0:T(8,128)S(1)} all-reduce(f32[16,256]{1,0:T(8,128)S(1)} %fusion.18), channel_id=1, replica_groups=mesh['row'=16,'col'=32] {'col'}, use_global_device_ids=true, to_apply=%region_8.9 | all-reduce | flops 4096 | bytes 32768 | tf_op jit(solution)/shard_map/psum | solution.py:109
  749.7 90.0 %psum.62 = f32[3,16,256]{2,1,0:T(8,128)S(1)} all-reduce(f32[3,16,256]{2,1,0:T(8,128)S(1)} %pad_maximum_fusion.1), channel_id=1, replica_groups=mesh['row'=16,'col'=32] {'col'}, use_global_device_ids=true, to_apply=%region_11.12 | all-reduce | flops 12288 | bytes 98304 | tf_op jit(solution)/shard_map/psum | solution.py:91
  839.7 1.8 slice_negate_fusion.1
  842.7 6.9 all-to-all-start.1
  851.7 4.2 all-to-all-done.1
  857.8 90.0 %psum.63 = f32[16,256]{1,0:T(8,128)S(1)} all-reduce(f32[16,256]{1,0:T(8,128)S(1)} %convolution_add_fusion), channel_id=1, replica_groups=mesh['row'=16,'col'=32] {'col'}, use_global_device_ids=true, to_apply=%region_12.13 | all-reduce | flops 4096 | bytes 32768 | tf_op jit(solution)/shard_map/psum | solution.py:109
  (105 shorter events, 37.6 us)
Async XLA Ops:
  7.2 40.8 %copy-start = (f32[768,384]{1,0:T(8,128)S(1)}, f32[768,384]{1,0:T(8,128)}, u32[]{:S(2)}) copy-start(f32[768,384]{1,0:T(8,128)} %param.23) | copy-start | bytes 3538948
  7.2 207.4 %all-reduce.9.cloned.1.call-start = ((), (), s32[]{:S(2)}) async-start(), calls=%async_computation.2 | async-start | bytes 786432
  50.2 278.4 %all-reduce.11.cloned.1.call-start = ((), (), s32[]{:S(2)}) async-start(), calls=%async_computation.3 | async-start | bytes 786432
  79.6 2.2 copy-start.11
  79.6 63.7 %copy-start.9 = (f32[1,768,8]{1,2,0:T(8,128)S(1)}, f32[1,768,8]{1,2,0:T(8,128)}, u32[]{:S(2)}) copy-start(f32[1,768,8]{1,2,0:T(8,128)} %get-tuple-element.118) | copy-start | bytes 73732
  208.2 3.9 copy-start.7
  213.0 1.5 copy-start.6
  214.5 2.2 copy-start.4
  214.5 3.2 copy-start.3
  214.5 3.1 copy-start.5
  216.6 236.4 %all-reduce.13.cloned.1.call-start = ((), (), s32[]{:S(2)}) async-start(), calls=%async_computation.4 | async-start | bytes 3932160
  330.5 0.7 copy-start.12
  330.5 215.6 %copy-start.10 = (f32[3,16,256]{2,1,0:T(8,128)S(1)}, f32[3,16,256]{2,1,0:T(8,128)}, u32[]{:S(2)}) copy-start(f32[3,16,256]{2,1,0:T(8,128)} %param.26) | copy-start | bytes 147460
  453.0 95.7 %copy-start.2 = (f32[392,256]{0,1:T(8,128)S(1)}, f32[392,256]{0,1:T(8,128)}, u32[]{:S(2)}) copy-start(f32[392,256]{0,1:T(8,128)} %get-tuple-element.114) | copy-start | bytes 1204228
  453.1 197.1 %copy-start.1 = (f32[392,256]{0,1:T(8,128)S(1)}, f32[392,256]{0,1:T(8,128)}, u32[]{:S(2)}) copy-start(f32[392,256]{0,1:T(8,128)} %get-tuple-element.115) | copy-start | bytes 1204228
  644.3 12.1 %all-to-all-start = ((f32[16,1,256]{2,1,0:T(1,128)}), f32[16,1,256]{2,1,0:T(1,128)S(1)}, u32[]{:S(2)}, u32[]{:S(2)}) async-start(f32[16,1,256]{2,1,0:T(1,128)} %reshape.358), calls=%async_computation | async-start | bytes 32768 | tf_op jit(solution)/shard_map/all_to_all | solution.py:97
  842.7 13.2 %all-to-all-start.1 = ((f32[16,1,512]{2,1,0:T(1,128)}), f32[16,1,512]{2,1,0:T(1,128)S(1)}, u32[]{:S(2)}, u32[]{:S(2)}) async-start(f32[16,1,512]{2,1,0:T(1,128)} %reshape.360), calls=%async_computation.1 | async-start | bytes 65536 | tf_op jit(solution)/shard_map/all_to_all | solution.py:97
  947.8 0.7 copy-start.8
Sparse Core Ops, SparseCore 0:
  50.3 111.0 all-reduce.8
  216.7 111.7 all-reduce.10
  332.3 120.6 all-reduce.12
where the time goes:
time: 956 us; the launch traced here: 955 us
  blocking collectives  641 us (67%)
  waiting for transfers between devices  231 us (24%)
  matrix products  22.4 us (2%)
  other arithmetic  16.9 us (2%)
  local copies, waits for them, and re-layouts  15.3 us (2%)
  between operations  14.8 us (2%)
  starting transfers between devices  12.9 us (1%)
    psum x3, blocking collectives, per_device(): totals = lax.psum(jnp.stack(parts), 'col')  272 us
    unnamed x6, waiting for transfers between devices  227 us
    psum x2, blocking collectives, per_device(): second_term = lax.psum(partial_sum, 'col')  180 us
    all_gather x3, blocking collectives, per_device(): lax.all_gather(sep_panels[current:current + 1], 'col', axis=2, tiled=True)  98.1 us
    all_gather x3, blocking collectives, per_device(): lax.all_gather(chain_panels[current:current + 1], 'col', axis=2, tiled=True)  91.6 us
  transfers between devices with their start and end apart: 5, of which 4 were waited for; matrix products, arithmetic and copies ran while one was open for 3% of the time, Pallas kernels for 0%

commit v1 on v0

--- a/solution.py
+++ b/solution.py
@@ -106,7 +106,7 @@
                 partial_sum = partial_sum + product(
                     mirror_cols, chain_colrows[pair_index(current, earlier)]
                 )
-            second_term = lax.psum(partial_sum, "col")
+            second_term = jnp.sum(lax.all_gather(partial_sum, "col"), axis=0)
             for earlier in range(current):
                 state = state.at[earlier, :, current * NB : (current + 1) * NB].set(
                     crossing[earlier]

time: 956 us -> 839 us (0.88)
  the two profiles are of different devices: /device:TPU:2 before, /device:TPU:1 now
where the time goes in v1:
time: 839 us; the launch traced here: 837 us
  blocking collectives  528 us (63%)
  waiting for transfers between devices  230 us (27%)
  matrix products  22.4 us (3%)
  other arithmetic  17 us (2%)
  local copies, waits for them, and re-layouts  15.3 us (2%)
  between operations  14.9 us (2%)
  starting transfers between devices  9.87 us (1%)
    psum x3, blocking collectives, per_device(): totals = lax.psum(jnp.stack(parts), 'col')  270 us
    unnamed x6, waiting for transfers between devices  225 us
    all_gather x3, blocking collectives, per_device(): lax.all_gather(sep_panels[current:current + 1], 'col', axis=2, tiled=True)  99.5 us
    all_gather x3, blocking collectives, per_device(): lax.all_gather(chain_panels[current:current + 1], 'col', axis=2, tiled=True)  91.6 us
    all_gather x2, blocking collectives, per_device(): second_term = jnp.sum(lax.all_gather(partial_sum, 'col'), axis=0)  66.6 us
  transfers between devices with their start and end apart: 5, of which 4 were waited for; matrix products, arithmetic and copies ran while one was open for 3% of the time, Pallas kernels for 0%

profile of v1, /device:TPU:1, one launch (start us, length us, event | category | flops | bytes accessed | tf_op | source)
XLA Modules:
  0.0 837.5 jit_solution(5409642843726919272)
XLA Ops:
  9.5 39.7 %all_gather.30 = f32[1,768,256]{1,2,0:T(8,128)S(1)} all-gather(f32[1,768,8]{1,2,0:T(8,128)S(1)} %get-tuple-element.119), channel_id=1, replica_groups=mesh['row'=16,'col'=32] {'col'}, dimensions={2}, use_global_device_ids=true | all-gather | bytes 811008 | tf_op jit(solution)/shard_map/all_gather | solution.py:57
  49.3 2.2 fusion.78
  51.6 29.2 %all_gather.33 = f32[1,768,256]{1,2,0:T(8,128)S(1)} all-gather(f32[1,768,8]{1,2,0:T(8,128)S(1)} %get-tuple-element.120), channel_id=1, replica_groups=mesh['row'=16,'col'=32] {'col'}, dimensions={2}, use_global_device_ids=true | all-gather | bytes 811008 | tf_op jit(solution)/shard_map/all_gather | solution.py:57
  81.0 2.2 fusion.80
  83.2 31.4 %all_gather.34 = f32[1,16,256]{1,2,0:T(8,128)} all-gather(f32[1,16,8]{1,2,0:T(8,128)S(1)} %get-tuple-element.131), channel_id=1, replica_groups=mesh['row'=16,'col'=32] {'col'}, dimensions={2}, use_global_device_ids=true | all-gather | bytes 16896 | tf_op jit(solution)/shard_map/all_gather | solution.py:58
  114.6 30.1 %all_gather.35 = f32[1,16,256]{1,2,0:T(8,128)} all-gather(f32[1,16,8]{1,2,0:T(8,128)S(1)} %get-tuple-element.130), channel_id=1, replica_groups=mesh['row'=16,'col'=32] {'col'}, dimensions={2}, use_global_device_ids=true | all-gather | bytes 16896 | tf_op jit(solution)/shard_map/all_gather | solution.py:58
  144.7 30.5 %all_gather.31 = f32[1,768,256]{1,2,0:T(8,128)S(1)} all-gather(f32[1,768,8]{1,2,0:T(8,128)S(1)} %copy-done.9), channel_id=1, replica_groups=mesh['row'=16,'col'=32] {'col'}, dimensions={2}, use_global_device_ids=true | all-gather | bytes 811008 | tf_op jit(solution)/shard_map/all_gather | solution.py:57
  175.3 30.1 %all_gather.32 = f32[1,16,256]{1,2,0:T(8,128)} all-gather(f32[1,16,8]{1,2,0:T(8,128)S(1)} %get-tuple-element.129), channel_id=1, replica_groups=mesh['row'=16,'col'=32] {'col'}, dimensions={2}, use_global_device_ids=true | all-gather | bytes 16896 | tf_op jit(solution)/shard_map/all_gather | solution.py:58
  211.5 1.9 maximum_select_fusion
  215.9 2.0 fusion.2
  220.2 107.6 %all-reduce.11.cloned.1.call-done = f32[256,384]{1,0:T(8,128)} async-done(((f32[256,384]{1,0:T(8,128)}), f32[256,384]{1,0:T(8,128)}) %all-reduce.11.cloned.1.call-update) | async-done | bytes 393232
  327.7 1.9 fusion
  330.4 3.2 and_reduce_fusion
  335.1 117.5 %all-reduce.13.cloned.1.call-done = (f32[256,384]{1,0:T(8,128)}, f32[392,256]{0,1:T(8,128)}, f32[392,256]{0,1:T(8,128)}, f32[392,256]{0,1:T(8,128)}) async-done(((f32[256,384]{1,0:T(8,128)}, f32[392,256]{0,1:T(8,128)}, f32[392,256]{0,1:T(8,128)}, f32[392,256]{0,1:T(8,128)}), (f32[256,384]{1,0:T(8,128)}, f32[392,256]{0,1:T(8,128)}, f32[392,256]{0,1:T(8,128)}, ...) | async-done | bytes 1597456
  454.1 90.6 %psum.43 = f32[1,16,256]{2,1,0:T(8,128)S(1)} all-reduce(f32[1,16,256]{2,1,0:T(8,128)S(1)} %convolution_bitcast_fusion.5), channel_id=1, replica_groups=mesh['row'=16,'col'=32] {'col'}, use_global_device_ids=true, to_apply=%region_4.5 | all-reduce | flops 4096 | bytes 32768 | tf_op jit(solution)/shard_map/psum | solution.py:91
  548.5 90.0 %psum.45 = f32[2,16,256]{2,1,0:T(8,128)S(1)} all-reduce(f32[2,16,256]{2,1,0:T(8,128)S(1)} %pad_maximum_fusion.2), channel_id=1, replica_groups=mesh['row'=16,'col'=32] {'col'}, use_global_device_ids=true, to_apply=%region_7.8 | all-reduce | flops 8192 | bytes 65536 | tf_op jit(solution)/shard_map/psum | solution.py:91
  638.6 2.0 slice_negate_fusion.2
  642.9 4.4 all-to-all-start
  656.0 33.5 %all-gather = f32[512,256]{1,0:T(8,128)S(1)} all-gather(f32[16,256]{1,0:T(8,128)S(1)} %fusion.18), channel_id=2, replica_groups=mesh['row'=16,'col'=32] {'col'}, dimensions={0}, use_global_device_ids=true | all-gather | bytes 540672 | tf_op jit(solution)/shard_map/all_gather | solution.py:109
  690.7 89.8 %psum.47 = f32[3,16,256]{2,1,0:T(8,128)S(1)} all-reduce(f32[3,16,256]{2,1,0:T(8,128)S(1)} %pad_maximum_fusion.1), channel_id=1, replica_groups=mesh['row'=16,'col'=32] {'col'}, use_global_device_ids=true, to_apply=%region_11.12 | all-reduce | flops 12288 | bytes 98304 | tf_op jit(solution)/shard_map/psum | solution.py:91
  780.5 1.8 slice_negate_fusion.1
  783.4 5.3 all-to-all-start.1
  790.8 4.4 all-to-all-done.1
  797.1 33.1 %all-gather.1 = f32[512,256]{1,0:T(8,128)S(1)} all-gather(f32[16,256]{1,0:T(8,128)S(1)} %convolution_add_fusion), channel_id=3, replica_groups=mesh['row'=16,'col'=32] {'col'}, dimensions={0}, use_global_device_ids=true | all-gather | bytes 540672 | tf_op jit(solution)/shard_map/all_gather | solution.py:109
  (107 shorter events, 37.9 us)
Async XLA Ops:
  7.2 42.1 %copy-start = (f32[768,384]{1,0:T(8,128)S(1)}, f32[768,384]{1,0:T(8,128)}, u32[]{:S(2)}) copy-start(f32[768,384]{1,0:T(8,128)} %param.23) | copy-start | bytes 3538948
  7.2 208.7 %all-reduce.9.cloned.1.call-start = ((), (), s32[]{:S(2)}) async-start(), calls=%async_computation.2 | async-start | bytes 786432
  51.5 276.2 %all-reduce.11.cloned.1.call-start = ((), (), s32[]{:S(2)}) async-start(), calls=%async_computation.3 | async-start | bytes 786432
  81.0 2.2 copy-start.11
  81.0 63.7 %copy-start.9 = (f32[1,768,8]{1,2,0:T(8,128)S(1)}, f32[1,768,8]{1,2,0:T(8,128)}, u32[]{:S(2)}) copy-start(f32[1,768,8]{1,2,0:T(8,128)} %get-tuple-element.118) | copy-start | bytes 73732
  209.5 3.9 copy-start.7
  214.4 1.5 copy-start.6
  215.8 2.2 copy-start.4
  215.8 3.2 copy-start.3
  215.8 3.1 copy-start.5
  217.9 234.7 %all-reduce.13.cloned.1.call-start = ((), (), s32[]{:S(2)}) async-start(), calls=%async_computation.4 | async-start | bytes 3932160
  329.7 0.7 copy-start.12
  329.7 215.1 %copy-start.10 = (f32[3,16,256]{2,1,0:T(8,128)S(1)}, f32[3,16,256]{2,1,0:T(8,128)}, u32[]{:S(2)}) copy-start(f32[3,16,256]{2,1,0:T(8,128)} %param.26) | copy-start | bytes 147460
  452.6 94.8 %copy-start.2 = (f32[392,256]{0,1:T(8,128)S(1)}, f32[392,256]{0,1:T(8,128)}, u32[]{:S(2)}) copy-start(f32[392,256]{0,1:T(8,128)} %get-tuple-element.114) | copy-start | bytes 1204228
  452.6 194.8 %copy-start.1 = (f32[392,256]{0,1:T(8,128)S(1)}, f32[392,256]{0,1:T(8,128)}, u32[]{:S(2)}) copy-start(f32[392,256]{0,1:T(8,128)} %get-tuple-element.115) | copy-start | bytes 1204228
  642.9 10.9 %all-to-all-start = ((f32[16,1,256]{2,1,0:T(1,128)}), f32[16,1,256]{2,1,0:T(1,128)S(1)}, u32[]{:S(2)}, u32[]{:S(2)}) async-start(f32[16,1,256]{2,1,0:T(1,128)} %reshape.354), calls=%async_computation | async-start | bytes 32768 | tf_op jit(solution)/shard_map/all_to_all | solution.py:97
  783.4 11.8 %all-to-all-start.1 = ((f32[16,1,512]{2,1,0:T(1,128)}), f32[16,1,512]{2,1,0:T(1,128)S(1)}, u32[]{:S(2)}, u32[]{:S(2)}) async-start(f32[16,1,512]{2,1,0:T(1,128)} %reshape.356), calls=%async_computation.1 | async-start | bytes 65536 | tf_op jit(solution)/shard_map/all_to_all | solution.py:97
  830.3 0.7 copy-start.8
Sparse Core Ops, SparseCore 0:
  51.6 109.0 all-reduce.8
  218.1 109.6 all-reduce.10
  331.5 121.0 all-reduce.12
